TPU v7x, 32 devices: a whole 2x2x4 slice. The times are simulated.
32 devices in a mesh: seg: 4 (over y, x), slab: 8 (over z, core).
Axes of the slice: x: 2, y: 2, z: 4, core: 2. Of those that a mesh axis runs over, the one named last changes fastest.
Arguments:
- positions: bfloat16 [4, 32, 3, 642], P('seg', 'slab'), may hold values from -6 to 6
- density: bfloat16 [4, 32, 3, 642], P('seg', 'slab'), may hold values from -6 to 6
- upsample: bfloat16 [642, 2562], replicated, may hold values from -0.25 to 0.25
- quad_weights: float32 [2562], replicated, may hold values from 0.3 to 3
- coarse_weights: float32 [642], replicated, may hold values from 0.3 to 3
- pair_target: int32 [4, 16], P('seg', 'slab'), may hold values from 0 to 3
- pair_source: int32 [4, 16], P('seg', 'slab'), may hold values from 0 to 7
- junction_cell: int32 [4, 8, 4], P('seg', 'slab'), may hold values from 0 to 3
- junction_target: int32 [4, 8, 4], P('seg', 'slab'), may hold values from 0 to 3
- wall_points: bfloat16 [4, 8, 3, 128], P('seg', 'slab'), may hold values from -6 to 6
- wall_traction: bfloat16 [4, 8, 3, 128], P('seg', 'slab'), may hold values from -6 to 6
- wall_near: int32 [4, 32, 2], P('seg', 'slab'), may hold values from 0 to 7
Outputs:
- velocity: float32 [4, 32, 3, 642], P('seg', 'slab')
All inputs are finite; a program needn't handle non-finite values.
Results may differ from a plain program's by a relative error of at most 0.0024.
Values may be sent and summed in bfloat16 or wider, within the bound.
A program may use at most 64 MiB of HBM per device.

v0:
```python
import math
import jax
import jax.numpy as jnp
from jax import lax
from jax.sharding import PartitionSpec as P

HALO = 2
EPSILON2 = 0.05
WALL_GAIN = 3.0


def with_halo(block, sides, width):
    for axis, dim in sides:
        count = lax.axis_size(axis)
        forward = [(i, i + 1) for i in range(count - 1)]
        backward = [(target, source) for source, target in forward]
        low = lax.ppermute(
            lax.slice_in_dim(block, block.shape[dim] - width, None, axis=dim), axis, forward
        )
        high = lax.ppermute(lax.slice_in_dim(block, 0, width, axis=dim), axis, backward)
        block = jnp.concatenate([low, block, high], axis=dim)
    return block


def kernel_rows(targets, sources, strength):
    offset = targets[:, :, None] - sources[:, None, :]
    distance2 = jnp.sum(offset * offset, axis=0)
    inverse = lax.rsqrt(distance2 + EPSILON2)
    inverse3 = inverse * inverse * inverse
    along_offset = jnp.sum(offset * strength[:, None, :], axis=0)
    summand = (
        strength[:, None, :] * (distance2 + 2.0 * EPSILON2) + along_offset[None] * offset
    ) * inverse3[None]
    return jnp.sum(summand, axis=2) / (8.0 * math.pi)


def stokes_block(targets, sources, strength):
    points = targets.shape[1]
    blocked = targets.reshape(3, 6, points // 6).transpose(1, 0, 2)
    result = lax.map(lambda target_rows: kernel_rows(target_rows, sources, strength), blocked)
    return result.transpose(1, 0, 2).reshape(3, points)


def add_to_cells(blocks, index, cell_count):
    onehot = (index[None, :] == jnp.arange(cell_count, dtype=jnp.int32)[:, None]).astype(
        jnp.float32
    )
    return jnp.einsum("cn,nkp->ckp", onehot, blocks, precision=lax.Precision.HIGHEST)


def local(
    positions,
    density,
    upsample,
    quad_weights,
    coarse_weights,
    pair_target,
    pair_source,
    junction_cell,
    junction_target,
    wall_points,
    wall_traction,
    wall_near,
):
    coarse_pos = positions[0]
    coarse_den = density[0]
    cell_count = coarse_pos.shape[0]
    rim_pos, rim_den = (
        with_halo(coarse_pos, (("slab", 0),), HALO),
        with_halo(coarse_den, (("slab", 0),), HALO),
    )
    fine_pos = jnp.einsum(
        "ckp,pq->ckq", rim_pos, upsample, preferred_element_type=jnp.float32
    ).astype(jnp.bfloat16)
    fine_den = jnp.einsum(
        "ckp,pq->ckq", rim_den, upsample, preferred_element_type=jnp.float32
    ).astype(jnp.bfloat16)
    targets = pair_target[0]
    sources = pair_source[0]

    def fine_pair(operands):
        target_pts, source_pts, source_den = operands
        strength = source_den.astype(jnp.float32) * quad_weights[None, :]
        return stokes_block(
            target_pts.astype(jnp.float32), source_pts.astype(jnp.float32), strength
        )

    local_blocks = lax.map(fine_pair, (coarse_pos[targets], fine_pos[sources], fine_den[sources]))
    velocity = add_to_cells(local_blocks, targets, cell_count)
    chosen = junction_cell[0, 0]
    arrived_pos, arrived_den = (
        lax.all_to_all(coarse_pos[chosen], "seg", split_axis=0, concat_axis=0, tiled=True),
        lax.all_to_all(coarse_den[chosen], "seg", split_axis=0, concat_axis=0, tiled=True),
    )
    goals = junction_target[0, 0]
    alive_mask = (jnp.arange(goals.shape[0], dtype=jnp.int32) != lax.axis_index("seg")).astype(
        jnp.float32
    )

    def coarse_pair(operands):
        target_pts, source_pts, source_den = operands
        strength = source_den.astype(jnp.float32) * coarse_weights[None, :]
        return stokes_block(
            target_pts.astype(jnp.float32), source_pts.astype(jnp.float32), strength
        )

    junction_blocks = (
        lax.map(coarse_pair, (coarse_pos[goals], arrived_pos, arrived_den))
        * alive_mask[:, None, None]
    )
    velocity = velocity + add_to_cells(junction_blocks, goals, cell_count)
    patch_pos, patch_trac = (
        lax.all_gather(wall_points[0], "slab", axis=0, tiled=True),
        lax.all_gather(wall_traction[0], "slab", axis=0, tiled=True),
    )
    near_rows = wall_near[0].reshape(-1)
    near_count = wall_near.shape[2]

    def wall_pair(operands):
        target_pts, source_pts, source_den = operands
        return stokes_block(
            target_pts.astype(jnp.float32),
            source_pts.astype(jnp.float32),
            source_den.astype(jnp.float32) * WALL_GAIN,
        )

    wall_blocks = lax.map(
        wall_pair,
        (jnp.repeat(coarse_pos, near_count, axis=0), patch_pos[near_rows], patch_trac[near_rows]),
    )
    velocity = velocity + jnp.sum(
        wall_blocks.reshape((cell_count, near_count) + wall_blocks.shape[1:]), axis=1
    )
    return velocity[None]


def solution(mesh):
    placed = (
        P("seg", "slab", None, None),
        P("seg", "slab", None, None),
        P(),
        P(),
        P(),
        P("seg", "slab"),
        P("seg", "slab"),
        P("seg", "slab", None),
        P("seg", "slab", None),
        P("seg", "slab", None, None),
        P("seg", "slab", None, None),
        P("seg", "slab", None),
    )
    return jax.shard_map(
        local, mesh=mesh, in_specs=placed, out_specs=P("seg", "slab", None, None), check_vma=False
    )
```

profile of v0, /device:TPU:0, one launch (start us, length us, event | category | flops | bytes accessed | tf_op | source)
XLA Modules:
  0.0 205.6 jit_solution(8631033830005076879)
XLA Ops:
  0.0 1.5 slice_bitcast_fusion.3
  1.5 3.0 %collective-permute-start = (bf16[2,3,642]{2,0,1:T(2,128)(2,1)}, bf16[2,3,642]{2,0,1:T(2,128)(2,1)}, u32[]{:S(2)}, u32[]{:S(2)}) collective-permute-start(bf16[2,3,642]{2,0,1:T(2,128)(2,1)} %get-tuple-element.324), channel_id=1, source_target_pairs={{0,1},{1,2},{2,3},{3,4},{4,5},{5,6},{6,7},{8,9},{9,10},{10,11},{11... | collective-permute-start | bytes 23120 | tf_op jit(solution)/shard_map/ppermute | solution.py:17
  5.8 1.4 slice_bitcast_fusion.1
  7.2 5.2 %collective-permute-start.2 = (bf16[2,3,642]{2,0,1:T(2,128)(2,1)}, bf16[2,3,642]{2,0,1:T(2,128)(2,1)}, u32[]{:S(2)}, u32[]{:S(2)}) collective-permute-start(bf16[2,3,642]{2,0,1:T(2,128)(2,1)} %get-tuple-element.322), channel_id=1, source_target_pairs={{0,1},{1,2},{2,3},{3,4},{4,5},{5,6},{6,7},{8,9},{9,10},{10,11},{11... | collective-permute-start | bytes 23120 | tf_op jit(solution)/shard_map/ppermute | solution.py:17
  16.3 3.9 %all-to-all-start = ((bf16[4,3,642]{2,1,0:T(4,128)(2,1)}), bf16[4,3,642]{2,1,0:T(4,128)(2,1)}, u32[]{:S(2)}, u32[]{:S(2)}) async-start(bf16[4,3,642]{2,1,0:T(4,128)(2,1)} %gather_fusion.4), calls=%async_computation | async-start | bytes 49152 | tf_op jit(solution)/shard_map/all_to_all | solution.py:92
  24.8 14.1 %all-gather = bf16[8,1,3,128]{3,2,1,0:T(4,128)(2,1)S(1)} all-gather(bf16[1,1,3,128]{3,2,1,0:T(4,128)(2,1)} %param.33), channel_id=2, replica_groups=mesh['seg'=4,'slab'=8] {'slab'}, dimensions={0}, use_global_device_ids=true | all-gather | bytes 6912 | tf_op jit(solution)/shard_map/all_gather | solution.py:113
  38.9 9.0 %all-gather.1 = bf16[8,1,3,128]{3,2,1,0:T(4,128)(2,1)S(1)} all-gather(bf16[1,1,3,128]{3,2,1,0:T(4,128)(2,1)} %param.34), channel_id=3, replica_groups=mesh['seg'=4,'slab'=8] {'slab'}, dimensions={0}, use_global_device_ids=true | all-gather | bytes 6912 | tf_op jit(solution)/shard_map/all_gather | solution.py:114
  50.2 37.8 %while.65 = (s32[]{:T(128)}, f32[8,3,642]{2,1,0:T(4,128)}, bf16[8,3,642]{2,1,0:T(4,128)(2,1)}, bf16[8,3,128]{2,1,0:T(4,128)(2,1)S(1)}, bf16[8,3,128]{2,1,0:T(4,128)(2,1)}, /*index=5*/s32[]{:T(128)}, s32[]{:T(128)}, s32[]{:T(128)}) while((s32[]{:T(128)}, f32[8,3,642]{2,1,0:T(4,128)}, bf16[8,3,642]{2,1,0:T(4,128)(2,1)}, ...), condition=%wide.region_20.21_spmd, body=%wide.region_14.20_spmd.sunk | while | flops 482442 | bytes 540622 | solution.py:127
  51.6 2.6 %while.68 = (s32[]{:T(128)}, f32[6,3,107]{2,1,0:T(4,128)S(1)}, f32[3,128]{1,0:T(4,128)S(1)}, f32[6,3,107]{2,0,1:T(8,128)S(1)}, f32[3,128]{1,0:T(4,128)S(1)}, /*index=5*/s32[]{:T(128)}) while((s32[]{:T(128)}, f32[6,3,107]{2,1,0:T(4,128)S(1)}, f32[3,128]{1,0:T(4,128)S(1)}, f32[6,3,107]{2,0,1:T(8,128)S(1)}, f32[3,128]{1,0:T(4,128)S(1)}, ...), condition=%wide.region_19.19_spmd, body=%wide.region_15.18_spmd.sunk | while | flops 479362 | bytes 457577 | solution.py:40
  56.4 2.6 %while.68 = (s32[]{:T(128)}, f32[6,3,107]{2,1,0:T(4,128)S(1)}, f32[3,128]{1,0:T(4,128)S(1)}, f32[6,3,107]{2,0,1:T(8,128)S(1)}, f32[3,128]{1,0:T(4,128)S(1)}, /*index=5*/s32[]{:T(128)}) while((s32[]{:T(128)}, f32[6,3,107]{2,1,0:T(4,128)S(1)}, f32[3,128]{1,0:T(4,128)S(1)}, f32[6,3,107]{2,0,1:T(8,128)S(1)}, f32[3,128]{1,0:T(4,128)S(1)}, ...), condition=%wide.region_19.19_spmd, body=%wide.region_15.18_spmd.sunk | while | flops 479362 | bytes 457577 | solution.py:40
  61.1 2.6 %while.68 = (s32[]{:T(128)}, f32[6,3,107]{2,1,0:T(4,128)S(1)}, f32[3,128]{1,0:T(4,128)S(1)}, f32[6,3,107]{2,0,1:T(8,128)S(1)}, f32[3,128]{1,0:T(4,128)S(1)}, /*index=5*/s32[]{:T(128)}) while((s32[]{:T(128)}, f32[6,3,107]{2,1,0:T(4,128)S(1)}, f32[3,128]{1,0:T(4,128)S(1)}, f32[6,3,107]{2,0,1:T(8,128)S(1)}, f32[3,128]{1,0:T(4,128)S(1)}, ...), condition=%wide.region_19.19_spmd, body=%wide.region_15.18_spmd.sunk | while | flops 479362 | bytes 457577 | solution.py:40
  65.8 2.6 %while.68 = (s32[]{:T(128)}, f32[6,3,107]{2,1,0:T(4,128)S(1)}, f32[3,128]{1,0:T(4,128)S(1)}, f32[6,3,107]{2,0,1:T(8,128)S(1)}, f32[3,128]{1,0:T(4,128)S(1)}, /*index=5*/s32[]{:T(128)}) while((s32[]{:T(128)}, f32[6,3,107]{2,1,0:T(4,128)S(1)}, f32[3,128]{1,0:T(4,128)S(1)}, f32[6,3,107]{2,0,1:T(8,128)S(1)}, f32[3,128]{1,0:T(4,128)S(1)}, ...), condition=%wide.region_19.19_spmd, body=%wide.region_15.18_spmd.sunk | while | flops 479362 | bytes 457577 | solution.py:40
  70.6 2.6 %while.68 = (s32[]{:T(128)}, f32[6,3,107]{2,1,0:T(4,128)S(1)}, f32[3,128]{1,0:T(4,128)S(1)}, f32[6,3,107]{2,0,1:T(8,128)S(1)}, f32[3,128]{1,0:T(4,128)S(1)}, /*index=5*/s32[]{:T(128)}) while((s32[]{:T(128)}, f32[6,3,107]{2,1,0:T(4,128)S(1)}, f32[3,128]{1,0:T(4,128)S(1)}, f32[6,3,107]{2,0,1:T(8,128)S(1)}, f32[3,128]{1,0:T(4,128)S(1)}, ...), condition=%wide.region_19.19_spmd, body=%wide.region_15.18_spmd.sunk | while | flops 479362 | bytes 457577 | solution.py:40
  75.3 2.6 %while.68 = (s32[]{:T(128)}, f32[6,3,107]{2,1,0:T(4,128)S(1)}, f32[3,128]{1,0:T(4,128)S(1)}, f32[6,3,107]{2,0,1:T(8,128)S(1)}, f32[3,128]{1,0:T(4,128)S(1)}, /*index=5*/s32[]{:T(128)}) while((s32[]{:T(128)}, f32[6,3,107]{2,1,0:T(4,128)S(1)}, f32[3,128]{1,0:T(4,128)S(1)}, f32[6,3,107]{2,0,1:T(8,128)S(1)}, f32[3,128]{1,0:T(4,128)S(1)}, ...), condition=%wide.region_19.19_spmd, body=%wide.region_15.18_spmd.sunk | while | flops 479362 | bytes 457577 | solution.py:40
  80.0 2.6 %while.68 = (s32[]{:T(128)}, f32[6,3,107]{2,1,0:T(4,128)S(1)}, f32[3,128]{1,0:T(4,128)S(1)}, f32[6,3,107]{2,0,1:T(8,128)S(1)}, f32[3,128]{1,0:T(4,128)S(1)}, /*index=5*/s32[]{:T(128)}) while((s32[]{:T(128)}, f32[6,3,107]{2,1,0:T(4,128)S(1)}, f32[3,128]{1,0:T(4,128)S(1)}, f32[6,3,107]{2,0,1:T(8,128)S(1)}, f32[3,128]{1,0:T(4,128)S(1)}, ...), condition=%wide.region_19.19_spmd, body=%wide.region_15.18_spmd.sunk | while | flops 479362 | bytes 457577 | solution.py:40
  84.8 2.6 %while.68 = (s32[]{:T(128)}, f32[6,3,107]{2,1,0:T(4,128)S(1)}, f32[3,128]{1,0:T(4,128)S(1)}, f32[6,3,107]{2,0,1:T(8,128)S(1)}, f32[3,128]{1,0:T(4,128)S(1)}, /*index=5*/s32[]{:T(128)}) while((s32[]{:T(128)}, f32[6,3,107]{2,1,0:T(4,128)S(1)}, f32[3,128]{1,0:T(4,128)S(1)}, f32[6,3,107]{2,0,1:T(8,128)S(1)}, f32[3,128]{1,0:T(4,128)S(1)}, ...), condition=%wide.region_19.19_spmd, body=%wide.region_15.18_spmd.sunk | while | flops 479362 | bytes 457577 | solution.py:40
  88.1 1.5 bitcast_reduce_fusion
  94.8 1.3 fusion.19
  98.9 2.2 %gather_fusion.1 = bf16[2,3,2562]{2,1,0:T(4,128)(2,1)} fusion(bf16[8,3,2562]{2,1,0:T(4,128)(2,1)} %copy.76, s32[1024]{0:T(1024)} %pad_clamp_fusion.3), kind=kCustom, calls=%fused_computation.1 | custom fusion | bytes 61496 | tf_op jit(solution)/shard_map/gather | solution.py:88
  101.2 2.2 %gather_fusion.2 = bf16[2,3,2562]{2,1,0:T(4,128)(2,1)} fusion(bf16[8,3,2562]{2,1,0:T(4,128)(2,1)} %copy.77, s32[1024]{0:T(1024)} %pad_clamp_fusion.3), kind=kCustom, calls=%fused_computation.2 | custom fusion | bytes 61496 | tf_op jit(solution)/shard_map/gather | solution.py:88
  103.4 47.6 %while.61 = (s32[]{:T(128)}, f32[2,3,642]{2,0,1:T(2,128)}, bf16[2,3,642]{2,1,0:T(4,128)(2,1)}, bf16[2,3,2562]{2,1,0:T(4,128)(2,1)}, bf16[2,3,2562]{2,1,0:T(4,128...) while((s32[]{:T(128)}, f32[2,3,642]{2,0,1:T(2,128)}, bf16[2,3,642]{2,1,0:T(4,128)(2,1)}, ...), condition=%wide.region_6.7_spmd, body=%wide.region_0.6_spmd.sunk | while | flops 9619678 | bytes 9207262 | solution.py:88
  104.2 1.4 bitcast_convert_fusion.6
  106.3 19.4 %while.66 = (s32[]{:T(128)}, f32[6,3,107]{2,1,0:T(4,128)S(1)}, f32[3,2562]{1,0:T(4,128)S(1)}, f32[6,3,107]{2,0,1:T(8,128)S(1)}, f32[3,2562]{1,0:T(4,128)}, /*index=5*/s32[]{:T(128)}) while((s32[]{:T(128)}, f32[6,3,107]{2,1,0:T(4,128)S(1)}, f32[3,2562]{1,0:T(4,128)S(1)}, f32[6,3,107]{2,0,1:T(8,128)S(1)}, f32[3,2562]{1,0:T(4,128)}, ...), condition=%wide.region_5.5_spmd, body=%wide.region_1.4_spmd.sunk | while | flops 9594692 | bytes 9031429 | solution.py:40
  106.3 1.9 fusion.64
  109.6 1.9 fusion.64
  112.8 1.9 fusion.64
  116.1 1.9 fusion.64
  119.3 1.9 fusion.64
  122.5 1.9 fusion.64
  125.8 1.4 dynamic_update_slice.33
  128.0 1.4 bitcast_convert_fusion.6
  130.1 19.4 %while.66 = (s32[]{:T(128)}, f32[6,3,107]{2,1,0:T(4,128)S(1)}, f32[3,2562]{1,0:T(4,128)S(1)}, f32[6,3,107]{2,0,1:T(8,128)S(1)}, f32[3,2562]{1,0:T(4,128)}, /*index=5*/s32[]{:T(128)}) while((s32[]{:T(128)}, f32[6,3,107]{2,1,0:T(4,128)S(1)}, f32[3,2562]{1,0:T(4,128)S(1)}, f32[6,3,107]{2,0,1:T(8,128)S(1)}, f32[3,2562]{1,0:T(4,128)}, ...), condition=%wide.region_5.5_spmd, body=%wide.region_1.4_spmd.sunk | while | flops 9594692 | bytes 9031429 | solution.py:40
  130.1 1.9 fusion.64
  133.4 1.9 fusion.64
  136.6 1.9 fusion.64
  139.9 1.9 fusion.64
  143.1 1.9 fusion.64
  146.3 1.9 fusion.64
  149.6 1.4 dynamic_update_slice.33
  151.0 4.1 %all-to-all-start.1 = ((bf16[4,3,642]{2,1,0:T(4,128)(2,1)}), bf16[4,3,642]{2,1,0:T(4,128)(2,1)}, u32[]{:S(2)}, u32[]{:S(2)}) async-start(bf16[4,3,642]{2,1,0:T(4,128)(2,1)} %gather_fusion.5), calls=%async_computation.1 | async-start | bytes 49152 | tf_op jit(solution)/shard_map/all_to_all | solution.py:93
  155.2 1.6 fusion.40
  156.8 3.2 %all-to-all-done.1 = bf16[4,3,642]{2,1,0:T(4,128)(2,1)} async-done(((bf16[4,3,642]{2,1,0:T(4,128)(2,1)}), bf16[4,3,642]{2,1,0:T(4,128)(2,1)}, u32[]{:S(2)}, u32[]{:S(2)}) %all-to-all-start.1) | async-done | bytes 15440 | tf_op jit(solution)/shard_map/all_to_all | solution.py:93
  160.0 43.1 %while.63 = (s32[]{:T(128)}, f32[4,3,642]{2,1,0:T(4,128)}, bf16[4,3,642]{2,1,0:T(4,128)(2,1)}, bf16[4,3,642]{2,1,0:T(4,128)(2,1)}, bf16[4,3,642]{2,1,0:T(4,128)(...) while((s32[]{:T(128)}, f32[4,3,642]{2,1,0:T(4,128)}, bf16[4,3,642]{2,1,0:T(4,128)(2,1)}, ...), condition=%wide.region_13.14_spmd, body=%wide.region_7.13_spmd.sunk | while | flops 2411998 | bytes 2346310 | solution.py:108
  162.2 7.9 %while.67 = (s32[]{:T(128)}, f32[6,3,107]{2,1,0:T(4,128)S(1)}, f32[3,642]{1,0:T(4,128)S(1)}, f32[6,3,107]{2,0,1:T(8,128)S(1)}, f32[3,642]{1,0:T(4,128)S(1)}, /*index=5*/s32[]{:T(128)}) while((s32[]{:T(128)}, f32[6,3,107]{2,1,0:T(4,128)S(1)}, f32[3,642]{1,0:T(4,128)S(1)}, f32[6,3,107]{2,0,1:T(8,128)S(1)}, f32[3,642]{1,0:T(4,128)S(1)}, ...), condition=%wide.region_12.12_spmd, body=%wide.region_8.11_spmd.sunk | while | flops 2404292 | bytes 2242185 | solution.py:40
  173.0 7.9 %while.67 = (s32[]{:T(128)}, f32[6,3,107]{2,1,0:T(4,128)S(1)}, f32[3,642]{1,0:T(4,128)S(1)}, f32[6,3,107]{2,0,1:T(8,128)S(1)}, f32[3,642]{1,0:T(4,128)S(1)}, /*index=5*/s32[]{:T(128)}) while((s32[]{:T(128)}, f32[6,3,107]{2,1,0:T(4,128)S(1)}, f32[3,642]{1,0:T(4,128)S(1)}, f32[6,3,107]{2,0,1:T(8,128)S(1)}, f32[3,642]{1,0:T(4,128)S(1)}, ...), condition=%wide.region_12.12_spmd, body=%wide.region_8.11_spmd.sunk | while | flops 2404292 | bytes 2242185 | solution.py:40
  183.7 7.9 %while.67 = (s32[]{:T(128)}, f32[6,3,107]{2,1,0:T(4,128)S(1)}, f32[3,642]{1,0:T(4,128)S(1)}, f32[6,3,107]{2,0,1:T(8,128)S(1)}, f32[3,642]{1,0:T(4,128)S(1)}, /*index=5*/s32[]{:T(128)}) while((s32[]{:T(128)}, f32[6,3,107]{2,1,0:T(4,128)S(1)}, f32[3,642]{1,0:T(4,128)S(1)}, f32[6,3,107]{2,0,1:T(8,128)S(1)}, f32[3,642]{1,0:T(4,128)S(1)}, ...), condition=%wide.region_12.12_spmd, body=%wide.region_8.11_spmd.sunk | while | flops 2404292 | bytes 2242185 | solution.py:40
  194.5 7.9 %while.67 = (s32[]{:T(128)}, f32[6,3,107]{2,1,0:T(4,128)S(1)}, f32[3,642]{1,0:T(4,128)S(1)}, f32[6,3,107]{2,0,1:T(8,128)S(1)}, f32[3,642]{1,0:T(4,128)S(1)}, /*index=5*/s32[]{:T(128)}) while((s32[]{:T(128)}, f32[6,3,107]{2,1,0:T(4,128)S(1)}, f32[3,642]{1,0:T(4,128)S(1)}, f32[6,3,107]{2,0,1:T(8,128)S(1)}, f32[3,642]{1,0:T(4,128)S(1)}, ...), condition=%wide.region_12.12_spmd, body=%wide.region_8.11_spmd.sunk | while | flops 2404292 | bytes 2242185 | solution.py:40
  204.0 1.6 fusion.26
  (670 shorter events, 117.1 us)
Async XLA Ops:
  0.0 94.8 %copy-start = (bf16[642,2562]{1,0:T(8,128)(2,1)S(1)}, bf16[642,2562]{1,0:T(8,128)(2,1)}, u32[]{:S(2)}) copy-start(bf16[642,2562]{1,0:T(8,128)(2,1)} %param.26) | copy-start | bytes 9868828
  1.5 93.3 %collective-permute-start = (bf16[2,3,642]{2,0,1:T(2,128)(2,1)}, bf16[2,3,642]{2,0,1:T(2,128)(2,1)}, u32[]{:S(2)}, u32[]{:S(2)}) collective-permute-start(bf16[2,3,642]{2,0,1:T(2,128)(2,1)} %get-tuple-element.324), channel_id=1, source_target_pairs={{0,1},{1,2},{2,3},{3,4},{4,5},{5,6},{6,7},{8,9},{9,10},{10,11},{11... | collective-permute-start | bytes 23120 | tf_op jit(solution)/shard_map/ppermute | solution.py:17
  4.5 90.3 %collective-permute-start.1 = (bf16[2,3,642]{2,0,1:T(2,128)(2,1)}, bf16[2,3,642]{2,0,1:T(2,128)(2,1)}, u32[]{:S(2)}, u32[]{:S(2)}) collective-permute-start(bf16[2,3,642]{2,0,1:T(2,128)(2,1)} %get-tuple-element.325), channel_id=1, source_target_pairs={{1,0},{2,1},{3,2},{4,3},{5,4},{6,5},{7,6},{9,8},{10,9},{11,10},{12... | collective-permute-start | bytes 23120 | tf_op jit(solution)/shard_map/ppermute | solution.py:20
  7.2 89.7 %collective-permute-start.2 = (bf16[2,3,642]{2,0,1:T(2,128)(2,1)}, bf16[2,3,642]{2,0,1:T(2,128)(2,1)}, u32[]{:S(2)}, u32[]{:S(2)}) collective-permute-start(bf16[2,3,642]{2,0,1:T(2,128)(2,1)} %get-tuple-element.322), channel_id=1, source_target_pairs={{0,1},{1,2},{2,3},{3,4},{4,5},{5,6},{6,7},{8,9},{9,10},{10,11},{11... | collective-permute-start | bytes 23120 | tf_op jit(solution)/shard_map/ppermute | solution.py:17
  12.4 84.4 %collective-permute-start.3 = (bf16[2,3,642]{2,0,1:T(2,128)(2,1)}, bf16[2,3,642]{2,0,1:T(2,128)(2,1)}, u32[]{:S(2)}, u32[]{:S(2)}) collective-permute-start(bf16[2,3,642]{2,0,1:T(2,128)(2,1)} %get-tuple-element.323), channel_id=1, source_target_pairs={{1,0},{2,1},{3,2},{4,3},{5,4},{6,5},{7,6},{9,8},{10,9},{11,10},{12... | collective-permute-start | bytes 23120 | tf_op jit(solution)/shard_map/ppermute | solution.py:20
  15.1 8.8 %copy-start.3 = (s32[1024]{0:T(1024)}, s32[1024]{0:T(1024)S(1)}, u32[]{:S(2)}) copy-start(s32[1024]{0:T(1024)S(1)} %pad_clamp_fusion.1) | copy-start | bytes 12292
  16.3 134.7 %all-to-all-start = ((bf16[4,3,642]{2,1,0:T(4,128)(2,1)}), bf16[4,3,642]{2,1,0:T(4,128)(2,1)}, u32[]{:S(2)}, u32[]{:S(2)}) async-start(bf16[4,3,642]{2,1,0:T(4,128)(2,1)} %gather_fusion.4), calls=%async_computation | async-start | bytes 49152 | tf_op jit(solution)/shard_map/all_to_all | solution.py:92
  88.1 8.8 %copy-start.2 = (bf16[1,4,3,642]{3,1,2,0:T(4,128)(2,1)S(1)}, bf16[1,4,3,642]{3,1,2,0:T(4,128)(2,1)}, u32[]{:S(2)}) copy-start(bf16[1,4,3,642]{3,1,2,0:T(4,128)(2,1)} %param.25) | copy-start | bytes 46228
  106.3 2.1 %copy-start.1 = (f32[3,2562]{1,0:T(4,128)S(1)}, f32[3,2562]{1,0:T(4,128)}, u32[]{:S(2)}) copy-start(f32[3,2562]{1,0:T(4,128)} %get-tuple-element.639) | copy-start | bytes 92236 | tf_op jit(solution)/shard_map/while/body/eval_jaxpr/while
  109.5 2.1 %copy-start.1 = (f32[3,2562]{1,0:T(4,128)S(1)}, f32[3,2562]{1,0:T(4,128)}, u32[]{:S(2)}) copy-start(f32[3,2562]{1,0:T(4,128)} %get-tuple-element.639) | copy-start | bytes 92236 | tf_op jit(solution)/shard_map/while/body/eval_jaxpr/while
  112.8 2.1 %copy-start.1 = (f32[3,2562]{1,0:T(4,128)S(1)}, f32[3,2562]{1,0:T(4,128)}, u32[]{:S(2)}) copy-start(f32[3,2562]{1,0:T(4,128)} %get-tuple-element.639) | copy-start | bytes 92236 | tf_op jit(solution)/shard_map/while/body/eval_jaxpr/while
  116.0 2.1 %copy-start.1 = (f32[3,2562]{1,0:T(4,128)S(1)}, f32[3,2562]{1,0:T(4,128)}, u32[]{:S(2)}) copy-start(f32[3,2562]{1,0:T(4,128)} %get-tuple-element.639) | copy-start | bytes 92236 | tf_op jit(solution)/shard_map/while/body/eval_jaxpr/while
  119.3 2.1 %copy-start.1 = (f32[3,2562]{1,0:T(4,128)S(1)}, f32[3,2562]{1,0:T(4,128)}, u32[]{:S(2)}) copy-start(f32[3,2562]{1,0:T(4,128)} %get-tuple-element.639) | copy-start | bytes 92236 | tf_op jit(solution)/shard_map/while/body/eval_jaxpr/while
  122.5 2.1 %copy-start.1 = (f32[3,2562]{1,0:T(4,128)S(1)}, f32[3,2562]{1,0:T(4,128)}, u32[]{:S(2)}) copy-start(f32[3,2562]{1,0:T(4,128)} %get-tuple-element.639) | copy-start | bytes 92236 | tf_op jit(solution)/shard_map/while/body/eval_jaxpr/while
  130.1 2.1 %copy-start.1 = (f32[3,2562]{1,0:T(4,128)S(1)}, f32[3,2562]{1,0:T(4,128)}, u32[]{:S(2)}) copy-start(f32[3,2562]{1,0:T(4,128)} %get-tuple-element.639) | copy-start | bytes 92236 | tf_op jit(solution)/shard_map/while/body/eval_jaxpr/while
  133.3 2.1 %copy-start.1 = (f32[3,2562]{1,0:T(4,128)S(1)}, f32[3,2562]{1,0:T(4,128)}, u32[]{:S(2)}) copy-start(f32[3,2562]{1,0:T(4,128)} %get-tuple-element.639) | copy-start | bytes 92236 | tf_op jit(solution)/shard_map/while/body/eval_jaxpr/while
  136.6 2.1 %copy-start.1 = (f32[3,2562]{1,0:T(4,128)S(1)}, f32[3,2562]{1,0:T(4,128)}, u32[]{:S(2)}) copy-start(f32[3,2562]{1,0:T(4,128)} %get-tuple-element.639) | copy-start | bytes 92236 | tf_op jit(solution)/shard_map/while/body/eval_jaxpr/while
  139.8 2.1 %copy-start.1 = (f32[3,2562]{1,0:T(4,128)S(1)}, f32[3,2562]{1,0:T(4,128)}, u32[]{:S(2)}) copy-start(f32[3,2562]{1,0:T(4,128)} %get-tuple-element.639) | copy-start | bytes 92236 | tf_op jit(solution)/shard_map/while/body/eval_jaxpr/while
  143.1 2.1 %copy-start.1 = (f32[3,2562]{1,0:T(4,128)S(1)}, f32[3,2562]{1,0:T(4,128)}, u32[]{:S(2)}) copy-start(f32[3,2562]{1,0:T(4,128)} %get-tuple-element.639) | copy-start | bytes 92236 | tf_op jit(solution)/shard_map/while/body/eval_jaxpr/while
  146.3 2.1 %copy-start.1 = (f32[3,2562]{1,0:T(4,128)S(1)}, f32[3,2562]{1,0:T(4,128)}, u32[]{:S(2)}) copy-start(f32[3,2562]{1,0:T(4,128)} %get-tuple-element.639) | copy-start | bytes 92236 | tf_op jit(solution)/shard_map/while/body/eval_jaxpr/while
  151.0 9.0 %all-to-all-start.1 = ((bf16[4,3,642]{2,1,0:T(4,128)(2,1)}), bf16[4,3,642]{2,1,0:T(4,128)(2,1)}, u32[]{:S(2)}, u32[]{:S(2)}) async-start(bf16[4,3,642]{2,1,0:T(4,128)(2,1)} %gather_fusion.5), calls=%async_computation.1 | async-start | bytes 49152 | tf_op jit(solution)/shard_map/all_to_all | solution.py:93
  160.0 43.1 %copy-start.5 = (f32[4]{0:T(128)S(1)}, f32[4]{0:T(128)}, u32[]{:S(2)}) copy-start(f32[4]{0:T(128)} %compare_convert_fusion) | copy-start | bytes 52
  160.0 44.0 %copy-start.4 = (s32[1,1,4]{2,1,0:T(1,128)S(1)}, s32[1,1,4]{2,1,0:T(1,128)}, u32[]{:S(2)}) copy-start(s32[1,1,4]{2,1,0:T(1,128)} %param.32) | copy-start | bytes 52
where the time goes:
time: 209 us; the launch traced here: 206 us
  other arithmetic  118 us (56%)
  local copies, waits for them, and re-layouts  31.9 us (15%)
  blocking collectives  23 us (11%)
  starting transfers between devices  18.8 us (9%)
  matrix products  5.87 us (3%)
  loops' own time  4.32 us (2%)
  waiting for transfers between devices  3.21 us (2%)
    reduce_sum x84, other arithmetic, kernel_rows(): along_offset = jnp.sum(offset * strength[:, None, :], axis=0)  42 us
    reduce_sum x84, other arithmetic, kernel_rows(): return jnp.sum(summand, axis=2) / (8.0 * math.pi)  37.9 us
    all_gather x1, blocking collectives, local(): lax.all_gather(wall_points[0], 'slab', axis=0, tiled=True)  14.1 us
    transpose x14, other arithmetic, stokes_block(): blocked = targets.reshape(3, 6, points // 6).transpose(1, 0, 2)  9.75 us
    all_gather x1, blocking collectives, local(): lax.all_gather(wall_traction[0], 'slab', axis=0, tiled=True)  8.97 us
    ppermute x2, starting transfers between devices, with_halo(): lax.ppermute(lax.slice_in_dim(block, block.shape[dim] - width, None, axis...  8.21 us
    mul x8, other arithmetic, wall_pair(): source_den.astype(jnp.float32) * WALL_GAIN  5.35 us
    add x84, other arithmetic, kernel_rows(): distance2 + 2.0 * EPSILON2  4.91 us
  transfers between devices with their start and end apart: 6, of which 1 were waited for; matrix products, arithmetic and copies ran while one was open for 54% of the time, Pallas kernels for 0%

commit v1 on v0

--- a/solution.py
+++ b/solution.py
@@ -7,6 +7,23 @@
 HALO = 2
 EPSILON2 = 0.05
 WALL_GAIN = 3.0
+
+
+def joined_along(parts, dim):
+    lengths = list(parts.shape[1:])
+    lengths[dim] *= parts.shape[0]
+    return jnp.moveaxis(parts, 0, dim).reshape(lengths)
+
+
+def collect(shard, axis, dim):
+    size = lax.axis_size(axis)
+    right = [(i, (i + 1) % size) for i in range(size)]
+    tiles = [shard]
+    while len(tiles) < size:
+        tiles.append(lax.ppermute(tiles[-1], axis, right))
+    place = lax.axis_index(axis)
+    tiles = jnp.stack(tiles)[(place - jnp.arange(size)) % size]
+    return joined_along(tiles, dim)
 
 
 def with_halo(block, sides, width):
@@ -110,7 +127,7 @@
     )
     velocity = velocity + add_to_cells(junction_blocks, goals, cell_count)
     patch_pos, patch_trac = (
-        lax.all_gather(wall_points[0], "slab", axis=0, tiled=True),
+        collect(wall_points[0], "slab", 0),
         lax.all_gather(wall_traction[0], "slab", axis=0, tiled=True),
     )
     near_rows = wall_near[0].reshape(-1)

time: 209 us -> 239 us (1.14)
  waiting for transfers between devices: 3.21 us -> 27.7 us
  blocking collectives: 23 us -> 11 us
  local copies, waits for them, and re-layouts: 31.9 us -> 40.5 us
  other arithmetic: 118 us -> 125 us
    ppermute x0 -> x7, waiting for transfers between devices: none -> 24.5 us  [collect(): tiles.append(lax.ppermute(tiles[-1], axis, right))]
    all_gather x1 -> x0, blocking collectives: 14.1 us -> none  [local(): lax.all_gather(wall_points[0], 'slab', axis=0, tiled=True)]
    dynamic_update_slice x84, other arithmetic: 1.09 us -> 8.03 us  [stokes_block(): lax.map(lambda target_rows: kernel_rows(target_rows, sources, strength),...]
    unnamed x11 -> x18, local copies, waits for them, and re-layouts: 0.78 us -> 6.11 us
    mul x8, other arithmetic: 5.35 us -> 0.03 us  [wall_pair(): source_den.astype(jnp.float32) * WALL_GAIN]
    convert_element_type x8, other arithmetic: 0.02 us -> 5.32 us  [wall_pair(): source_pts.astype(jnp.float32)]
  transfers between devices with their start and end apart: 6 -> 13, of which waited for: 1 -> 7; matrix products, arithmetic and copies ran while one was open for 54% -> 53% of each run, Pallas kernels for 0% -> 0%
where the time goes in v1:
time: 239 us; the launch traced here: 235 us
  other arithmetic  125 us (52%)
  local copies, waits for them, and re-layouts  40.5 us (17%)
  waiting for transfers between devices  27.7 us (12%)
  starting transfers between devices  21 us (9%)
  blocking collectives  11 us (5%)
  matrix products  5.85 us (2%)
  loops' own time  3.85 us (2%)
    reduce_sum x84, other arithmetic, kernel_rows(): along_offset = jnp.sum(offset * strength[:, None, :], axis=0)  42 us
    reduce_sum x84, other arithmetic, kernel_rows(): return jnp.sum(summand, axis=2) / (8.0 * math.pi)  37.9 us
    ppermute x7, waiting for transfers between devices, collect(): tiles.append(lax.ppermute(tiles[-1], axis, right))  24.5 us
    all_gather x1, blocking collectives, local(): lax.all_gather(wall_traction[0], 'slab', axis=0, tiled=True)  11 us
    transpose x14, other arithmetic, stokes_block(): blocked = targets.reshape(3, 6, points // 6).transpose(1, 0, 2)  9.76 us
    ppermute x2, starting transfers between devices, with_halo(): lax.ppermute(lax.slice_in_dim(block, block.shape[dim] - width, None, axis...  8.85 us
    dynamic_update_slice x84, other arithmetic, stokes_block(): lax.map(lambda target_rows: kernel_rows(target_rows, sources, strength),...  8.03 us
    unnamed x18, local copies, waits for them, and re-layouts  6.11 us
  transfers between devices with their start and end apart: 13, of which 7 were waited for; matrix products, arithmetic and copies ran while one was open for 53% of the time, Pallas kernels for 0%

profile of v1, /device:TPU:0, one launch (start us, length us, event | category | flops | bytes accessed | tf_op | source)
XLA Modules:
  0.0 235.3 jit_solution(18344794213525686322)
XLA Ops:
  0.0 1.5 slice_bitcast_fusion.3
  2.8 3.6 %collective-permute-start = (bf16[2,3,642]{2,0,1:T(2,128)(2,1)}, bf16[2,3,642]{2,0,1:T(2,128)(2,1)}, u32[]{:S(2)}, u32[]{:S(2)}) collective-permute-start(bf16[2,3,642]{2,0,1:T(2,128)(2,1)} %get-tuple-element.324), channel_id=1, source_target_pairs={{0,1},{1,2},{2,3},{3,4},{4,5},{5,6},{6,7},{8,9},{9,10},{10,11},{11... | collective-permute-start | bytes 23120 | tf_op jit(solution)/shard_map/ppermute | solution.py:34
  6.4 1.4 slice_bitcast_fusion.1
  9.1 5.2 %collective-permute-start.2 = (bf16[2,3,642]{2,0,1:T(2,128)(2,1)}, bf16[2,3,642]{2,0,1:T(2,128)(2,1)}, u32[]{:S(2)}, u32[]{:S(2)}) collective-permute-start(bf16[2,3,642]{2,0,1:T(2,128)(2,1)} %get-tuple-element.322), channel_id=1, source_target_pairs={{0,1},{1,2},{2,3},{3,4},{4,5},{5,6},{6,7},{8,9},{9,10},{10,11},{11... | collective-permute-start | bytes 23120 | tf_op jit(solution)/shard_map/ppermute | solution.py:34
  18.1 3.9 %all-to-all-start = ((bf16[4,3,642]{2,1,0:T(4,128)(2,1)}), bf16[4,3,642]{2,1,0:T(4,128)(2,1)}, u32[]{:S(2)}, u32[]{:S(2)}) async-start(bf16[4,3,642]{2,1,0:T(4,128)(2,1)} %gather_fusion.4), calls=%async_computation | async-start | bytes 49152 | tf_op jit(solution)/shard_map/all_to_all | solution.py:109
  26.6 11.0 %all-gather = bf16[8,1,3,128]{3,2,1,0:T(4,128)(2,1)S(1)} all-gather(bf16[1,1,3,128]{3,2,1,0:T(4,128)(2,1)} %param.34), channel_id=2, replica_groups=mesh['seg'=4,'slab'=8] {'slab'}, dimensions={0}, use_global_device_ids=true | all-gather | bytes 6912 | tf_op jit(solution)/shard_map/all_gather | solution.py:131
  46.0 3.4 %collective-permute-done.5 = bf16[1,3,128]{2,1,0:T(4,128)(2,1)S(1)} collective-permute-done((bf16[1,3,128]{2,1,0:T(4,128)(2,1)}, bf16[1,3,128]{2,1,0:T(4,128)(2,1)S(1)}, u32[]{:S(2)}, u32[]{:S(2)}) %collective-permute-start.5) | collective-permute-done | bytes 800 | tf_op jit(solution)/shard_map/ppermute | solution.py:23
  50.0 4.2 %collective-permute-done.6 = bf16[1,3,128]{2,1,0:T(4,128)(2,1)S(1)} collective-permute-done((bf16[1,3,128]{2,1,0:T(4,128)(2,1)S(1)}, bf16[1,3,128]{2,1,0:T(4,128)(2,1)S(1)}, u32[]{:S(2)}, u32[]{:S(2)}) %collective-permute-start.6) | collective-permute-done | bytes 800 | tf_op jit(solution)/shard_map/ppermute | solution.py:23
  54.7 4.3 %collective-permute-done.7 = bf16[1,3,128]{2,1,0:T(4,128)(2,1)S(1)} collective-permute-done((bf16[1,3,128]{2,1,0:T(4,128)(2,1)S(1)}, bf16[1,3,128]{2,1,0:T(4,128)(2,1)S(1)}, u32[]{:S(2)}, u32[]{:S(2)}) %collective-permute-start.7) | collective-permute-done | bytes 800 | tf_op jit(solution)/shard_map/ppermute | solution.py:23
  59.6 4.2 %collective-permute-done.8 = bf16[1,3,128]{2,1,0:T(4,128)(2,1)S(1)} collective-permute-done((bf16[1,3,128]{2,1,0:T(4,128)(2,1)S(1)}, bf16[1,3,128]{2,1,0:T(4,128)(2,1)S(1)}, u32[]{:S(2)}, u32[]{:S(2)}) %collective-permute-start.8) | collective-permute-done | bytes 800 | tf_op jit(solution)/shard_map/ppermute | solution.py:23
  64.4 4.2 %collective-permute-done.9 = bf16[1,3,128]{2,1,0:T(4,128)(2,1)S(1)} collective-permute-done((bf16[1,3,128]{2,1,0:T(4,128)(2,1)S(1)}, bf16[1,3,128]{2,1,0:T(4,128)(2,1)S(1)}, u32[]{:S(2)}, u32[]{:S(2)}) %collective-permute-start.9) | collective-permute-done | bytes 800 | tf_op jit(solution)/shard_map/ppermute | solution.py:23
  69.2 4.2 %collective-permute-done.10 = bf16[1,3,128]{2,1,0:T(4,128)(2,1)S(1)} collective-permute-done((bf16[1,3,128]{2,1,0:T(4,128)(2,1)S(1)}, bf16[1,3,128]{2,1,0:T(4,128)(2,1)S(1)}, u32[]{:S(2)}, u32[]{:S(2)}) %collective-permute-start.10) | collective-permute-done | bytes 800 | tf_op jit(solution)/shard_map/ppermute | solution.py:23
  77.3 37.8 %while.65 = (s32[]{:T(128)}, f32[8,3,642]{2,1,0:T(4,128)}, bf16[8,3,642]{2,1,0:T(4,128)(2,1)}, bf16[8,3,128]{2,1,0:T(4,128)(2,1)}, bf16[8,3,128]{2,1,0:T(4,128)(2,1)S(1)}, /*index=5*/s32[]{:T(128)}, s32[]{:T(128)}, s32[]{:T(128)}) while((s32[]{:T(128)}, f32[8,3,642]{2,1,0:T(4,128)}, bf16[8,3,642]{2,1,0:T(4,128)(2,1)}, ...), condition=%wide.region_20.21_spmd, body=%wide.region_14.20_spmd.sunk | while | flops 482442 | bytes 540130 | solution.py:144
  78.8 2.6 %while.68 = (s32[]{:T(128)}, f32[6,3,107]{2,1,0:T(4,128)S(1)}, f32[3,128]{1,0:T(4,128)S(1)}, f32[6,3,107]{2,0,1:T(8,128)S(1)}, f32[3,128]{1,0:T(4,128)S(1)}, /*index=5*/s32[]{:T(128)}) while((s32[]{:T(128)}, f32[6,3,107]{2,1,0:T(4,128)S(1)}, f32[3,128]{1,0:T(4,128)S(1)}, f32[6,3,107]{2,0,1:T(8,128)S(1)}, f32[3,128]{1,0:T(4,128)S(1)}, ...), condition=%wide.region_19.19_spmd, body=%wide.region_15.18_spmd.sunk | while | flops 479362 | bytes 457585 | solution.py:57
  83.5 2.6 %while.68 = (s32[]{:T(128)}, f32[6,3,107]{2,1,0:T(4,128)S(1)}, f32[3,128]{1,0:T(4,128)S(1)}, f32[6,3,107]{2,0,1:T(8,128)S(1)}, f32[3,128]{1,0:T(4,128)S(1)}, /*index=5*/s32[]{:T(128)}) while((s32[]{:T(128)}, f32[6,3,107]{2,1,0:T(4,128)S(1)}, f32[3,128]{1,0:T(4,128)S(1)}, f32[6,3,107]{2,0,1:T(8,128)S(1)}, f32[3,128]{1,0:T(4,128)S(1)}, ...), condition=%wide.region_19.19_spmd, body=%wide.region_15.18_spmd.sunk | while | flops 479362 | bytes 457585 | solution.py:57
  88.2 2.6 %while.68 = (s32[]{:T(128)}, f32[6,3,107]{2,1,0:T(4,128)S(1)}, f32[3,128]{1,0:T(4,128)S(1)}, f32[6,3,107]{2,0,1:T(8,128)S(1)}, f32[3,128]{1,0:T(4,128)S(1)}, /*index=5*/s32[]{:T(128)}) while((s32[]{:T(128)}, f32[6,3,107]{2,1,0:T(4,128)S(1)}, f32[3,128]{1,0:T(4,128)S(1)}, f32[6,3,107]{2,0,1:T(8,128)S(1)}, f32[3,128]{1,0:T(4,128)S(1)}, ...), condition=%wide.region_19.19_spmd, body=%wide.region_15.18_spmd.sunk | while | flops 479362 | bytes 457585 | solution.py:57
  93.0 2.6 %while.68 = (s32[]{:T(128)}, f32[6,3,107]{2,1,0:T(4,128)S(1)}, f32[3,128]{1,0:T(4,128)S(1)}, f32[6,3,107]{2,0,1:T(8,128)S(1)}, f32[3,128]{1,0:T(4,128)S(1)}, /*index=5*/s32[]{:T(128)}) while((s32[]{:T(128)}, f32[6,3,107]{2,1,0:T(4,128)S(1)}, f32[3,128]{1,0:T(4,128)S(1)}, f32[6,3,107]{2,0,1:T(8,128)S(1)}, f32[3,128]{1,0:T(4,128)S(1)}, ...), condition=%wide.region_19.19_spmd, body=%wide.region_15.18_spmd.sunk | while | flops 479362 | bytes 457585 | solution.py:57
  97.7 2.6 %while.68 = (s32[]{:T(128)}, f32[6,3,107]{2,1,0:T(4,128)S(1)}, f32[3,128]{1,0:T(4,128)S(1)}, f32[6,3,107]{2,0,1:T(8,128)S(1)}, f32[3,128]{1,0:T(4,128)S(1)}, /*index=5*/s32[]{:T(128)}) while((s32[]{:T(128)}, f32[6,3,107]{2,1,0:T(4,128)S(1)}, f32[3,128]{1,0:T(4,128)S(1)}, f32[6,3,107]{2,0,1:T(8,128)S(1)}, f32[3,128]{1,0:T(4,128)S(1)}, ...), condition=%wide.region_19.19_spmd, body=%wide.region_15.18_spmd.sunk | while | flops 479362 | bytes 457585 | solution.py:57
  102.4 2.6 %while.68 = (s32[]{:T(128)}, f32[6,3,107]{2,1,0:T(4,128)S(1)}, f32[3,128]{1,0:T(4,128)S(1)}, f32[6,3,107]{2,0,1:T(8,128)S(1)}, f32[3,128]{1,0:T(4,128)S(1)}, /*index=5*/s32[]{:T(128)}) while((s32[]{:T(128)}, f32[6,3,107]{2,1,0:T(4,128)S(1)}, f32[3,128]{1,0:T(4,128)S(1)}, f32[6,3,107]{2,0,1:T(8,128)S(1)}, f32[3,128]{1,0:T(4,128)S(1)}, ...), condition=%wide.region_19.19_spmd, body=%wide.region_15.18_spmd.sunk | while | flops 479362 | bytes 457585 | solution.py:57
  107.1 2.6 %while.68 = (s32[]{:T(128)}, f32[6,3,107]{2,1,0:T(4,128)S(1)}, f32[3,128]{1,0:T(4,128)S(1)}, f32[6,3,107]{2,0,1:T(8,128)S(1)}, f32[3,128]{1,0:T(4,128)S(1)}, /*index=5*/s32[]{:T(128)}) while((s32[]{:T(128)}, f32[6,3,107]{2,1,0:T(4,128)S(1)}, f32[3,128]{1,0:T(4,128)S(1)}, f32[6,3,107]{2,0,1:T(8,128)S(1)}, f32[3,128]{1,0:T(4,128)S(1)}, ...), condition=%wide.region_19.19_spmd, body=%wide.region_15.18_spmd.sunk | while | flops 479362 | bytes 457585 | solution.py:57
  111.8 2.6 %while.68 = (s32[]{:T(128)}, f32[6,3,107]{2,1,0:T(4,128)S(1)}, f32[3,128]{1,0:T(4,128)S(1)}, f32[6,3,107]{2,0,1:T(8,128)S(1)}, f32[3,128]{1,0:T(4,128)S(1)}, /*index=5*/s32[]{:T(128)}) while((s32[]{:T(128)}, f32[6,3,107]{2,1,0:T(4,128)S(1)}, f32[3,128]{1,0:T(4,128)S(1)}, f32[6,3,107]{2,0,1:T(8,128)S(1)}, f32[3,128]{1,0:T(4,128)S(1)}, ...), condition=%wide.region_19.19_spmd, body=%wide.region_15.18_spmd.sunk | while | flops 479362 | bytes 457585 | solution.py:57
  115.1 1.5 bitcast_reduce_fusion
  120.8 2.2 gather_fusion.1
  123.0 2.2 gather_fusion.2
  125.2 55.5 %while.61 = (s32[]{:T(128)}, f32[2,3,642]{2,0,1:T(2,128)}, bf16[2,3,642]{2,1,0:T(4,128)(2,1)}, bf16[2,3,2562]{2,1,0:T(4,128)(2,1)}, bf16[2,3,2562]{2,1,0:T(4,128...) while((s32[]{:T(128)}, f32[2,3,642]{2,0,1:T(2,128)}, bf16[2,3,642]{2,1,0:T(4,128)(2,1)}, ...), condition=%wide.region_6.7_spmd, body=%wide.region_0.6_spmd.sunk | while | flops 9619678 | bytes 9206514 | solution.py:105
  128.1 22.7 %while.66 = (s32[]{:T(128)}, f32[6,3,107]{2,1,0:T(4,128)}, f32[3,2562]{1,0:T(4,128)S(1)}, f32[6,3,107]{2,0,1:T(8,128)S(1)}, f32[3,2562]{1,0:T(4,128)}, /*index=5*/s32[]{:T(128)}) while((s32[]{:T(128)}, f32[6,3,107]{2,1,0:T(4,128)}, f32[3,2562]{1,0:T(4,128)S(1)}, f32[6,3,107]{2,0,1:T(8,128)S(1)}, f32[3,2562]{1,0:T(4,128)}, ...), condition=%wide.region_5.5_spmd, body=%wide.region_1.4_spmd.sunk | while | flops 9594692 | bytes 9030673 | solution.py:57
  128.2 1.9 fusion.66
  131.9 1.9 fusion.66
  135.7 1.9 fusion.66
  139.5 1.9 fusion.66
  143.3 1.9 fusion.66
  147.1 1.9 fusion.66
  155.9 22.7 %while.66 = (s32[]{:T(128)}, f32[6,3,107]{2,1,0:T(4,128)}, f32[3,2562]{1,0:T(4,128)S(1)}, f32[6,3,107]{2,0,1:T(8,128)S(1)}, f32[3,2562]{1,0:T(4,128)}, /*index=5*/s32[]{:T(128)}) while((s32[]{:T(128)}, f32[6,3,107]{2,1,0:T(4,128)}, f32[3,2562]{1,0:T(4,128)S(1)}, f32[6,3,107]{2,0,1:T(8,128)S(1)}, f32[3,2562]{1,0:T(4,128)}, ...), condition=%wide.region_5.5_spmd, body=%wide.region_1.4_spmd.sunk | while | flops 9594692 | bytes 9030673 | solution.py:57
  155.9 1.9 fusion.66
  159.7 1.9 fusion.66
  163.5 1.9 fusion.66
  167.3 1.9 fusion.66
  171.1 1.9 fusion.66
  174.9 1.9 fusion.66
  180.8 4.1 %all-to-all-start.1 = ((bf16[4,3,642]{2,1,0:T(4,128)(2,1)}), bf16[4,3,642]{2,1,0:T(4,128)(2,1)}, u32[]{:S(2)}, u32[]{:S(2)}) async-start(bf16[4,3,642]{2,1,0:T(4,128)(2,1)} %gather_fusion.5), calls=%async_computation.1 | async-start | bytes 49152 | tf_op jit(solution)/shard_map/all_to_all | solution.py:110
  184.9 1.6 fusion.40
  186.6 3.2 %all-to-all-done.1 = bf16[4,3,642]{2,1,0:T(4,128)(2,1)} async-done(((bf16[4,3,642]{2,1,0:T(4,128)(2,1)}), bf16[4,3,642]{2,1,0:T(4,128)(2,1)}, u32[]{:S(2)}, u32[]{:S(2)}) %all-to-all-start.1) | async-done | bytes 15440 | tf_op jit(solution)/shard_map/all_to_all | solution.py:110
  189.8 43.1 %while.63 = (s32[]{:T(128)}, f32[4,3,642]{2,1,0:T(4,128)}, bf16[4,3,642]{2,1,0:T(4,128)(2,1)}, bf16[4,3,642]{2,1,0:T(4,128)(2,1)}, bf16[4,3,642]{2,1,0:T(4,128)(...) while((s32[]{:T(128)}, f32[4,3,642]{2,1,0:T(4,128)}, bf16[4,3,642]{2,1,0:T(4,128)(2,1)}, ...), condition=%wide.region_13.14_spmd, body=%wide.region_7.13_spmd.sunk | while | flops 2411998 | bytes 2345818 | solution.py:125
  192.0 7.9 %while.67 = (s32[]{:T(128)}, f32[6,3,107]{2,1,0:T(4,128)S(1)}, f32[3,642]{1,0:T(4,128)S(1)}, f32[6,3,107]{2,0,1:T(8,128)S(1)}, f32[3,642]{1,0:T(4,128)S(1)}, /*index=5*/s32[]{:T(128)}) while((s32[]{:T(128)}, f32[6,3,107]{2,1,0:T(4,128)S(1)}, f32[3,642]{1,0:T(4,128)S(1)}, f32[6,3,107]{2,0,1:T(8,128)S(1)}, f32[3,642]{1,0:T(4,128)S(1)}, ...), condition=%wide.region_12.12_spmd, body=%wide.region_8.11_spmd.sunk | while | flops 2404292 | bytes 2242193 | solution.py:57
  202.7 7.9 %while.67 = (s32[]{:T(128)}, f32[6,3,107]{2,1,0:T(4,128)S(1)}, f32[3,642]{1,0:T(4,128)S(1)}, f32[6,3,107]{2,0,1:T(8,128)S(1)}, f32[3,642]{1,0:T(4,128)S(1)}, /*index=5*/s32[]{:T(128)}) while((s32[]{:T(128)}, f32[6,3,107]{2,1,0:T(4,128)S(1)}, f32[3,642]{1,0:T(4,128)S(1)}, f32[6,3,107]{2,0,1:T(8,128)S(1)}, f32[3,642]{1,0:T(4,128)S(1)}, ...), condition=%wide.region_12.12_spmd, body=%wide.region_8.11_spmd.sunk | while | flops 2404292 | bytes 2242193 | solution.py:57
  213.5 7.9 %while.67 = (s32[]{:T(128)}, f32[6,3,107]{2,1,0:T(4,128)S(1)}, f32[3,642]{1,0:T(4,128)S(1)}, f32[6,3,107]{2,0,1:T(8,128)S(1)}, f32[3,642]{1,0:T(4,128)S(1)}, /*index=5*/s32[]{:T(128)}) while((s32[]{:T(128)}, f32[6,3,107]{2,1,0:T(4,128)S(1)}, f32[3,642]{1,0:T(4,128)S(1)}, f32[6,3,107]{2,0,1:T(8,128)S(1)}, f32[3,642]{1,0:T(4,128)S(1)}, ...), condition=%wide.region_12.12_spmd, body=%wide.region_8.11_spmd.sunk | while | flops 2404292 | bytes 2242193 | solution.py:57
  224.3 7.9 %while.67 = (s32[]{:T(128)}, f32[6,3,107]{2,1,0:T(4,128)S(1)}, f32[3,642]{1,0:T(4,128)S(1)}, f32[6,3,107]{2,0,1:T(8,128)S(1)}, f32[3,642]{1,0:T(4,128)S(1)}, /*index=5*/s32[]{:T(128)}) while((s32[]{:T(128)}, f32[6,3,107]{2,1,0:T(4,128)S(1)}, f32[3,642]{1,0:T(4,128)S(1)}, f32[6,3,107]{2,0,1:T(8,128)S(1)}, f32[3,642]{1,0:T(4,128)S(1)}, ...), condition=%wide.region_12.12_spmd, body=%wide.region_8.11_spmd.sunk | while | flops 2404292 | bytes 2242193 | solution.py:57
  233.7 1.6 fusion.26
  (693 shorter events, 141.0 us)
Async XLA Ops:
  0.0 116.6 %copy-start = (bf16[642,2562]{1,0:T(8,128)(2,1)S(1)}, bf16[642,2562]{1,0:T(8,128)(2,1)}, u32[]{:S(2)}) copy-start(bf16[642,2562]{1,0:T(8,128)(2,1)} %param.26) | copy-start | bytes 9868828
  1.5 115.1 %collective-permute-start.1 = (bf16[2,3,642]{2,0,1:T(2,128)(2,1)}, bf16[2,3,642]{2,0,1:T(2,128)(2,1)}, u32[]{:S(2)}, u32[]{:S(2)}) collective-permute-start(bf16[2,3,642]{2,0,1:T(2,128)(2,1)} %get-tuple-element.325), channel_id=1, source_target_pairs={{1,0},{2,1},{3,2},{4,3},{5,4},{6,5},{7,6},{9,8},{10,9},{11,10},{12... | collective-permute-start | bytes 23120 | tf_op jit(solution)/shard_map/ppermute | solution.py:37
  2.8 113.8 %collective-permute-start = (bf16[2,3,642]{2,0,1:T(2,128)(2,1)}, bf16[2,3,642]{2,0,1:T(2,128)(2,1)}, u32[]{:S(2)}, u32[]{:S(2)}) collective-permute-start(bf16[2,3,642]{2,0,1:T(2,128)(2,1)} %get-tuple-element.324), channel_id=1, source_target_pairs={{0,1},{1,2},{2,3},{3,4},{4,5},{5,6},{6,7},{8,9},{9,10},{10,11},{11... | collective-permute-start | bytes 23120 | tf_op jit(solution)/shard_map/ppermute | solution.py:34
  7.8 110.9 %collective-permute-start.3 = (bf16[2,3,642]{2,0,1:T(2,128)(2,1)}, bf16[2,3,642]{2,0,1:T(2,128)(2,1)}, u32[]{:S(2)}, u32[]{:S(2)}) collective-permute-start(bf16[2,3,642]{2,0,1:T(2,128)(2,1)} %get-tuple-element.323), channel_id=1, source_target_pairs={{1,0},{2,1},{3,2},{4,3},{5,4},{6,5},{7,6},{9,8},{10,9},{11,10},{12... | collective-permute-start | bytes 23120 | tf_op jit(solution)/shard_map/ppermute | solution.py:37
  9.1 109.6 %collective-permute-start.2 = (bf16[2,3,642]{2,0,1:T(2,128)(2,1)}, bf16[2,3,642]{2,0,1:T(2,128)(2,1)}, u32[]{:S(2)}, u32[]{:S(2)}) collective-permute-start(bf16[2,3,642]{2,0,1:T(2,128)(2,1)} %get-tuple-element.322), channel_id=1, source_target_pairs={{0,1},{1,2},{2,3},{3,4},{4,5},{5,6},{6,7},{8,9},{9,10},{10,11},{11... | collective-permute-start | bytes 23120 | tf_op jit(solution)/shard_map/ppermute | solution.py:34
  14.3 30.0 %collective-permute-start.4 = (bf16[1,3,128]{2,1,0:T(4,128)(2,1)}, bf16[1,3,128]{2,1,0:T(4,128)(2,1)}, u32[]{:S(2)}, u32[]{:S(2)}) collective-permute-start(bf16[1,3,128]{2,1,0:T(4,128)(2,1)} %bitcast.163), channel_id=1, source_target_pairs={{0,1},{1,2},{2,3},{3,4},{4,5},{5,6},{6,7},{7,0},{8,9},{9,10},{10,1... | collective-permute-start | bytes 2312 | tf_op jit(solution)/shard_map/ppermute | solution.py:23
  18.1 162.7 %all-to-all-start = ((bf16[4,3,642]{2,1,0:T(4,128)(2,1)}), bf16[4,3,642]{2,1,0:T(4,128)(2,1)}, u32[]{:S(2)}, u32[]{:S(2)}) async-start(bf16[4,3,642]{2,1,0:T(4,128)(2,1)} %gather_fusion.4), calls=%async_computation | async-start | bytes 49152 | tf_op jit(solution)/shard_map/all_to_all | solution.py:109
  44.3 5.1 %collective-permute-start.5 = (bf16[1,3,128]{2,1,0:T(4,128)(2,1)}, bf16[1,3,128]{2,1,0:T(4,128)(2,1)S(1)}, u32[]{:S(2)}, u32[]{:S(2)}) collective-permute-start(bf16[1,3,128]{2,1,0:T(4,128)(2,1)} %collective-permute-done.4), channel_id=1, source_target_pairs={{0,1},{1,2},{2,3},{3,4},{4,5},{5,6},{6,7},{7,0},{8,9},{9,10},{10,1... | collective-permute-start | bytes 2312 | tf_op jit(solution)/shard_map/ppermute | solution.py:23
  49.4 4.8 %collective-permute-start.6 = (bf16[1,3,128]{2,1,0:T(4,128)(2,1)S(1)}, bf16[1,3,128]{2,1,0:T(4,128)(2,1)S(1)}, u32[]{:S(2)}, u32[]{:S(2)}) collective-permute-start(bf16[1,3,128]{2,1,0:T(4,128)(2,1)S(1)} %collective-permute-done.5), channel_id=1, source_target_pairs={{0,1},{1,2},{2,3},{3,4},{4,5},{5,6},{6,7},{7,0},{8,9},{9,10},{10,1... | collective-permute-start | bytes 2312 | tf_op jit(solution)/shard_map/ppermute | solution.py:23
  54.2 4.8 %collective-permute-start.7 = (bf16[1,3,128]{2,1,0:T(4,128)(2,1)S(1)}, bf16[1,3,128]{2,1,0:T(4,128)(2,1)S(1)}, u32[]{:S(2)}, u32[]{:S(2)}) collective-permute-start(bf16[1,3,128]{2,1,0:T(4,128)(2,1)S(1)} %collective-permute-done.6), channel_id=1, source_target_pairs={{0,1},{1,2},{2,3},{3,4},{4,5},{5,6},{6,7},{7,0},{8,9},{9,10},{10,1... | collective-permute-start | bytes 2312 | tf_op jit(solution)/shard_map/ppermute | solution.py:23
  59.0 4.8 %collective-permute-start.8 = (bf16[1,3,128]{2,1,0:T(4,128)(2,1)S(1)}, bf16[1,3,128]{2,1,0:T(4,128)(2,1)S(1)}, u32[]{:S(2)}, u32[]{:S(2)}) collective-permute-start(bf16[1,3,128]{2,1,0:T(4,128)(2,1)S(1)} %collective-permute-done.7), channel_id=1, source_target_pairs={{0,1},{1,2},{2,3},{3,4},{4,5},{5,6},{6,7},{7,0},{8,9},{9,10},{10,1... | collective-permute-start | bytes 2312 | tf_op jit(solution)/shard_map/ppermute | solution.py:23
  63.8 4.8 %collective-permute-start.9 = (bf16[1,3,128]{2,1,0:T(4,128)(2,1)S(1)}, bf16[1,3,128]{2,1,0:T(4,128)(2,1)S(1)}, u32[]{:S(2)}, u32[]{:S(2)}) collective-permute-start(bf16[1,3,128]{2,1,0:T(4,128)(2,1)S(1)} %collective-permute-done.8), channel_id=1, source_target_pairs={{0,1},{1,2},{2,3},{3,4},{4,5},{5,6},{6,7},{7,0},{8,9},{9,10},{10,1... | collective-permute-start | bytes 2312 | tf_op jit(solution)/shard_map/ppermute | solution.py:23
  68.6 4.8 %collective-permute-start.10 = (bf16[1,3,128]{2,1,0:T(4,128)(2,1)S(1)}, bf16[1,3,128]{2,1,0:T(4,128)(2,1)S(1)}, u32[]{:S(2)}, u32[]{:S(2)}) collective-permute-start(bf16[1,3,128]{2,1,0:T(4,128)(2,1)S(1)} %collective-permute-done.9), channel_id=1, source_target_pairs={{0,1},{1,2},{2,3},{3,4},{4,5},{5,6},{6,7},{7,0},{8,9},{9,10},{10,1... | collective-permute-start | bytes 2312 | tf_op jit(solution)/shard_map/ppermute | solution.py:23
  77.3 39.4 %copy-start.2 = (bf16[1,4,3,642]{3,1,2,0:T(4,128)(2,1)S(1)}, bf16[1,4,3,642]{3,1,2,0:T(4,128)(2,1)}, u32[]{:S(2)}) copy-start(bf16[1,4,3,642]{3,1,2,0:T(4,128)(2,1)} %param.24) | copy-start | bytes 46228
  115.1 3.6 %copy-start.3 = (bf16[1,4,3,642]{3,1,2,0:T(4,128)(2,1)S(1)}, bf16[1,4,3,642]{3,1,2,0:T(4,128)(2,1)}, u32[]{:S(2)}) copy-start(bf16[1,4,3,642]{3,1,2,0:T(4,128)(2,1)} %param.25) | copy-start | bytes 46228
  128.1 2.1 copy-start.1
  131.9 2.1 copy-start.1
  135.7 2.1 copy-start.1
  139.5 2.1 copy-start.1
  143.3 2.1 copy-start.1
  147.1 2.1 copy-start.1
  155.9 2.1 copy-start.1
  159.7 2.1 copy-start.1
  163.5 2.1 copy-start.1
  167.2 2.1 copy-start.1
  171.0 2.1 copy-start.1
  174.8 2.1 copy-start.1
  180.8 9.0 %all-to-all-start.1 = ((bf16[4,3,642]{2,1,0:T(4,128)(2,1)}), bf16[4,3,642]{2,1,0:T(4,128)(2,1)}, u32[]{:S(2)}, u32[]{:S(2)}) async-start(bf16[4,3,642]{2,1,0:T(4,128)(2,1)} %gather_fusion.5), calls=%async_computation.1 | async-start | bytes 49152 | tf_op jit(solution)/shard_map/all_to_all | solution.py:110
  189.8 43.1 %copy-start.5 = (f32[4]{0:T(128)S(1)}, f32[4]{0:T(128)}, u32[]{:S(2)}) copy-start(f32[4]{0:T(128)} %compare_convert_fusion) | copy-start | bytes 52
  189.8 44.0 %copy-start.4 = (s32[1,1,4]{2,1,0:T(1,128)S(1)}, s32[1,1,4]{2,1,0:T(1,128)}, u32[]{:S(2)}) copy-start(s32[1,1,4]{2,1,0:T(1,128)} %param.32) | copy-start | bytes 52
